TPU v7x, 32 devices: a whole 2x2x4 slice. The times are simulated.
32 devices in a mesh: tm: 16 (over z, y, core), band: 2 (over x).
Axes of the slice: x: 2, y: 2, z: 4, core: 2. Of those that a mesh axis runs over, the one named last changes fastest.
Arguments:
- phonon: float32 [32, 256, 256], P('tm', 'band'), may hold values from -4 to 4
- momentum: float32 [32, 256, 256], P('tm', 'band'), may hold values from -6 to 6
- source: float32 [32, 256, 256], P('tm', 'band'), may hold values from -6 to 6
- guess: float32 [32, 256, 256], P('tm', 'band'), may hold values from -4 to 4
- bonds: int32 [2, 256, 256], P(None, 'band'), may hold values 0 or 1
Outputs:
- solution: float32 [32, 256, 256], P('tm', 'band')
- momentum_new: float32 [32, 256, 256], P('tm', 'band')
All inputs are finite; a program needn't handle non-finite values. No bound on the sum of `bonds` on one device may be relied on, other than what follows from the above.
Results may differ from a plain program's by a relative error of at most 0.000064.
Values sent between devices are 32-bit elements; how exact they have to be, the bound alone decides.
No kernel may reach another device: no remote copies, remote signals or barrier semaphores. Data moves between devices by JAX's collectives and lax.ppermute only.
A program may use at most 64 MiB of HBM per device.

v0:
```python
import math
import jax
import jax.numpy as jnp
from jax import lax
from jax.sharding import PartitionSpec as P

ORDER = 24
hop_angle = 0.3
coupling = 0.2
stiffness = 1.0
mass_term = 0.5
relaxation = 0.25
step_size = 0.25
cheb_base = 4.03
cheb_slope = 0.5
half_width = 4.0
deep_width = 4


def extended(value, sides, width):
    for axis, dim in sides:
        size, length = (lax.axis_size(axis), value.shape[dim])
        up = [(i, (i + 1) % size) for i in range(size)]
        down = [(j, i) for i, j in up]
        last = lax.slice_in_dim(value, length - width, length, axis=dim)
        leading = lax.slice_in_dim(value, 0, width, axis=dim)
        before = lax.ppermute(last, axis, up)
        after = lax.ppermute(leading, axis, down)
        value = jnp.concatenate([before, value, after], axis=dim)
    return value


def passed_along(value, axis, by):
    size = lax.axis_size(axis)
    return lax.ppermute(value, axis, [(i, (i + by) % size) for i in range(size)])


def dft_basis(length_total):
    rows = lax.broadcasted_iota(jnp.int32, (length_total, length_total), 0)
    columns = lax.broadcasted_iota(jnp.int32, (length_total, length_total), 1)
    phase = (2 * (rows // 2) + 1) * columns % (2 * length_total)
    angle = phase.astype(jnp.float32) * (math.pi / length_total)
    return math.sqrt(2.0 / length_total) * jnp.where(rows % 2 == 0, jnp.cos(angle), jnp.sin(angle))


def cheb_centre(index, length_total):
    angle = (2 * (index // 2) + 1).astype(jnp.float32) * (math.pi / length_total)
    return cheb_base + cheb_slope * (1.0 - jnp.cos(angle))


def pair_tables(horizontal, vertical, vertical_prev, row_even, column_even):
    horizontal_prev = jnp.roll(horizontal, 1, 1)
    vertical_up = jnp.roll(vertical, 1, 0)
    strengths = (
        jnp.where(column_even, horizontal, horizontal_prev),
        jnp.where(column_even, horizontal_prev, horizontal),
        jnp.where(row_even, vertical, vertical_up),
        jnp.where(row_even, vertical_prev, vertical),
    )
    return tuple(
        ((jnp.cosh(hop_angle * strength), jnp.sinh(hop_angle * strength)) for strength in strengths)
    )


def partner_of(vector, colour, row_even, column_even):
    if colour == 0:
        return jnp.where(column_even, jnp.roll(vector, -1, 2), jnp.roll(vector, 1, 2))
    if colour == 1:
        return jnp.where(column_even, jnp.roll(vector, 1, 2), jnp.roll(vector, -1, 2))
    if colour == 2:
        return jnp.where(row_even, jnp.roll(vector, -1, 1), jnp.roll(vector, 1, 1))
    padded = extended(vector, (("band", 1),), 1)
    return jnp.where(row_even, padded[:, :-2], padded[:, 2:])


def to_spectrum(piece):
    basis = dft_basis(piece.shape[0])
    return jnp.einsum("kl,lrc->krc", basis, piece, precision=lax.Precision.HIGHEST)


def to_slices(piece):
    basis = dft_basis(piece.shape[0])
    return jnp.einsum("kl,krc->lrc", basis, piece, precision=lax.Precision.HIGHEST)


def shards(phonon, momentum, source, guess, bonds):
    slice_count, row_count, col_count = guess.shape
    cycle_size = lax.axis_size("tm")
    position = lax.axis_index("tm")
    grid_shape = (row_count, col_count)
    row_even = lax.broadcasted_iota(jnp.int32, grid_shape, 0) % 2 == 0
    column_even = lax.broadcasted_iota(jnp.int32, grid_shape, 1) % 2 == 0
    edge_bonds = passed_along(bonds[1][-1:], "band", 1)
    vertical_prev = jnp.concatenate([edge_bonds, bonds[1][:-1]], 0)
    tables = pair_tables(
        bonds[0].astype(jnp.float32),
        bonds[1].astype(jnp.float32),
        vertical_prev.astype(jnp.float32),
        row_even,
        column_even,
    )

    def apply_pairs(vector, colours):
        for colour in colours:
            cosh_part, sinh_part = tables[colour]
            vector = cosh_part * vector + sinh_part * partner_of(
                vector, colour, row_even, column_even
            )
        return vector

    phonon_rims = extended(phonon, (("tm", 0),), 1)
    factor_wide = jnp.exp(-coupling * phonon_rims)
    expo = factor_wide[1:-1]
    first_sign = jnp.where(position == 0, -1.0, 1.0).astype(jnp.float32)
    last_sign = jnp.where(position == cycle_size - 1, -1.0, 1.0).astype(jnp.float32)

    def from_prev(piece):
        return passed_along(piece, "tm", 1) * first_sign

    def from_after(piece):
        return passed_along(piece, "tm", -1) * last_sign

    applied = apply_pairs(expo * guess, (0, 1, 2, 3))
    link = guess - jnp.concatenate([from_prev(applied[-1:]), applied[:-1]], 0)
    shifted = jnp.concatenate([link[1:], from_after(link[:1])], 0)
    normal = link - expo * apply_pairs(shifted, (3, 2, 1, 0))
    residual = source - normal
    mixed = to_spectrum(lax.all_to_all(residual, "tm", split_axis=1, concat_axis=0, tiled=True))
    spectrum = lax.all_to_all(mixed, "tm", split_axis=0, concat_axis=1, tiled=True)
    freq_index = position * slice_count + jnp.arange(slice_count, dtype=jnp.int32)
    centre = cheb_centre(freq_index, slice_count * cycle_size)[:, None, None]
    ratio = centre / half_width
    start = (jnp.zeros_like(spectrum), spectrum, spectrum / centre, 1.0 / ratio)

    def sweep_block(counter, carry):
        accum, remaining, direction, weight_now = carry
        stacked = extended(jnp.stack([remaining, direction]), (("band", 2),), deep_width)
        rem_wide = stacked[0]
        dir_wide = stacked[1]
        for inner in range(deep_width):
            offset = deep_width - inner
            middle = dir_wide[:, 1:-1]
            beside_all = (
                dir_wide[:, :-2]
                + dir_wide[:, 2:]
                + jnp.roll(middle, 1, 2)
                + jnp.roll(middle, -1, 2)
            )
            accum = accum + dir_wide[:, offset : offset + row_count]
            rem_wide = rem_wide[:, 1:-1] - (centre * middle - beside_all)
            weight_new = 1.0 / (2.0 * ratio - weight_now)
            dir_wide = weight_new * weight_now * middle + 2.0 * weight_new / half_width * rem_wide
            weight_now = weight_new
        return (accum, rem_wide, dir_wide, weight_now)

    accum = lax.fori_loop(0, ORDER // deep_width, sweep_block, start)[0]
    mixed_back = to_slices(lax.all_to_all(accum, "tm", split_axis=1, concat_axis=0, tiled=True))
    timed = lax.all_to_all(mixed_back, "tm", split_axis=0, concat_axis=1, tiled=True)
    solution = guess + relaxation * timed
    propagated = apply_pairs(expo * solution, (0, 1, 2, 3))
    image = solution - jnp.concatenate([from_prev(propagated[-1:]), propagated[:-1]], 0)
    pulled = apply_pairs(jnp.concatenate([image[1:], from_after(image[:1])], 0), (3, 2, 1, 0))
    fermion_force = -2.0 * coupling * expo * solution * pulled
    boson_force = (
        stiffness * (2.0 * phonon - phonon_rims[:-2] - phonon_rims[2:]) + mass_term * phonon
    )
    momentum_new = momentum - step_size * (boson_force + fermion_force)
    return (solution, momentum_new)


def solution(mesh):
    return jax.shard_map(
        shards,
        mesh=mesh,
        in_specs=(
            P("tm", "band", None),
            P("tm", "band", None),
            P("tm", "band", None),
            P("tm", "band", None),
            P(None, "band", None),
        ),
        out_specs=(P("tm", "band", None), P("tm", "band", None)),
        check_vma=False,
    )
```

profile of v0, /device:TPU:0, one launch (start us, length us, event | category | flops | bytes accessed | tf_op | source)
XLA Modules:
  0.0 157.5 jit_solution(9558485487474373816)
XLA Ops:
  0.6 0.7 slice_bitcast_fusion.4
  1.3 3.0 %collective-permute-start.2 = (s32[1,256]{1,0:T(1,128)S(1)}, s32[1,256]{1,0:T(1,128)S(1)}, u32[]{:S(2)}, u32[]{:S(2)}) collective-permute-start(s32[1,256]{1,0:T(1,128)S(1)} %slice_bitcast_fusion.4), channel_id=1, source_target_pairs={{0,1},{1,0},{2,3},{3,2},{4,5},{5,4},{6,7},{7,6},{8,9},{9,8},{10,11... | collective-permute-start | bytes 3080 | tf_op jit(solution)/shard_map/ppermute | solution.py:35
  4.3 1.0 fusion.157
  5.4 4.4 %collective-permute-start.4 = (f32[1,128,256]{2,1,0:T(8,128)S(1)}, f32[1,128,256]{2,1,0:T(8,128)S(1)}, u32[]{:S(2)}, u32[]{:S(2)}) collective-permute-start(f32[1,128,256]{2,1,0:T(8,128)S(1)} %get-tuple-element.314), channel_id=1, source_target_pairs={{2,0},{4,2},{6,4},{8,6},{10,8},{12,10},{14,12},{16,14},{18,16},{20... | collective-permute-start | bytes 393224 | tf_op jit(solution)/shard_map/ppermute | solution.py:28
  10.9 1.7 %collective-permute-done.3 = f32[1,128,256]{2,1,0:T(8,128)S(1)} collective-permute-done((f32[1,128,256]{2,1,0:T(8,128)S(1)}, f32[1,128,256]{2,1,0:T(8,128)S(1)}, u32[]{:S(2)}, u32[]{:S(2)}) %collective-permute-start.3) | collective-permute-done | bytes 131104 | tf_op jit(solution)/shard_map/ppermute | solution.py:27
  13.7 2.0 %collective-permute-start.6 = (f32[2,1,256]{2,1,0:T(1,128)S(1)}, f32[2,1,256]{2,1,0:T(1,128)S(1)}, u32[]{:S(2)}, u32[]{:S(2)}) collective-permute-start(f32[2,1,256]{2,1,0:T(1,128)S(1)} %get-tuple-element.298), channel_id=1, source_target_pairs={{1,0},{0,1},{3,2},{2,3},{5,4},{4,5},{7,6},{6,7},{9,8},{8,9},{11,10... | collective-permute-start | bytes 6152 | tf_op jit(solution)/shard_map/ppermute | solution.py:28
  15.7 1.6 collective-permute-done.5
  17.5 7.1 %collective-permute-done.7 = f32[1,128,256]{2,1,0:T(8,128)S(1)} collective-permute-done((f32[1,128,256]{2,1,0:T(8,128)S(1)}, f32[1,128,256]{2,1,0:T(8,128)S(1)}, u32[]{:S(2)}, u32[]{:S(2)}) %collective-permute-start.7) | collective-permute-done | bytes 131104 | tf_op jit(solution)/shard_map/ppermute | solution.py:35
  24.8 2.5 %collective-permute-done.8 = f32[1,128,256]{2,1,0:T(8,128)S(1)} collective-permute-done((f32[1,128,256]{2,1,0:T(8,128)S(1)}, f32[1,128,256]{2,1,0:T(8,128)S(1)}, u32[]{:S(2)}, u32[]{:S(2)}) %collective-permute-start.8) | collective-permute-done | bytes 131104 | tf_op jit(solution)/shard_map/ppermute | solution.py:35
  27.3 2.0 %collective-permute-start.9 = (f32[2,1,256]{2,1,0:T(1,128)S(1)}, f32[2,1,256]{2,1,0:T(1,128)S(1)}, u32[]{:S(2)}, u32[]{:S(2)}) collective-permute-start(f32[2,1,256]{2,1,0:T(1,128)S(1)} %get-tuple-element.291), channel_id=1, source_target_pairs={{0,1},{1,0},{2,3},{3,2},{4,5},{5,4},{6,7},{7,6},{8,9},{9,8},{10,11... | collective-permute-start | bytes 6152 | tf_op jit(solution)/shard_map/ppermute | solution.py:27
  29.5 1.5 collective-permute-done.9
  31.0 2.0 %collective-permute-done.10 = f32[2,1,256]{2,1,0:T(1,128)S(1)} collective-permute-done((f32[2,1,256]{2,1,0:T(1,128)S(1)}, f32[2,1,256]{2,1,0:T(1,128)S(1)}, u32[]{:S(2)}, u32[]{:S(2)}) %collective-permute-start.10) | collective-permute-done | bytes 2080 | tf_op jit(solution)/shard_map/ppermute | solution.py:28
  33.9 0.8 copy-done.4
  35.0 0.9 copy.43
  35.9 4.5 %all-to-all-start = ((f32[2,128,256]{2,0,1:T(2,128)}), f32[2,128,256]{2,0,1:T(2,128)S(1)}, u32[]{:S(2)}, u32[]{:S(2)}) async-start(f32[2,128,256]{2,0,1:T(2,128)} %copy.43), calls=%async_computation | async-start | bytes 524288 | tf_op jit(solution)/shard_map/all_to_all | solution.py:128
  40.4 10.0 %all-to-all-done = f32[2,128,256]{2,0,1:T(2,128)S(1)} async-done(((f32[2,128,256]{2,0,1:T(2,128)}), f32[2,128,256]{2,0,1:T(2,128)S(1)}, u32[]{:S(2)}, u32[]{:S(2)}) %all-to-all-start) | async-done | bytes 262176 | tf_op jit(solution)/shard_map/all_to_all | solution.py:128
  50.7 0.5 fusion.90
  51.2 0.9 copy.46
  52.0 3.5 %all-to-all-start.1 = ((f32[32,8,256]{2,1,0:T(8,128)}), f32[32,8,256]{2,1,0:T(8,128)S(1)}, u32[]{:S(2)}, u32[]{:S(2)}) async-start(f32[32,8,256]{2,1,0:T(8,128)} %copy.46), calls=%async_computation.1 | async-start | bytes 524288 | tf_op jit(solution)/shard_map/all_to_all | solution.py:129
  55.7 9.8 %all-to-all-done.1 = f32[32,8,256]{2,1,0:T(8,128)S(1)} async-done(((f32[32,8,256]{2,1,0:T(8,128)}), f32[32,8,256]{2,1,0:T(8,128)S(1)}, u32[]{:S(2)}, u32[]{:S(2)}) %all-to-all-start.1) | async-done | bytes 262176 | tf_op jit(solution)/shard_map/all_to_all | solution.py:129
  65.7 42.2 %while.22 = (s32[]{:T(128)}, f32[2,128,256]{2,1,0:T(8,128)S(1)}, f32[2,128,256]{2,1,0:T(8,128)S(1)}, f32[2,128,256]{2,1,0:T(8,128)S(1)}, f32[2,1,1]{0,2,1:T(1,12...) while((s32[]{:T(128)}, f32[2,128,256]{2,1,0:T(8,128)S(1)}, ...), condition=%wide.region_1.2_spmd.clone.clone.clone, body=%wide.region_0.1_spmd.clone.clone.clone.sunk | while | flops 3704962 | bytes 17105376 | solution.py:156
  66.1 1.7 %collective-permute-start.1 = (f32[2,2,4,256]{3,2,1,0:T(4,128)S(1)}, f32[2,2,4,256]{3,2,1,0:T(4,128)S(1)}, u32[]{:S(2)}, u32[]{:S(2)}) collective-permute-start(f32[2,2,4,256]{3,2,1,0:T(4,128)S(1)} %get-tuple-element.405), channel_id=1, source_target_pairs={{0,1},{1,0},{2,3},{3,2},{4,5},{5,4},{6,7},{7,6},{8,9},{9,8},{10,11... | collective-permute-start | bytes 49160 | tf_op jit(solution)/shard_map/while/body/eval_jaxpr/ppermute | solution.py:27
  68.0 1.5 collective-permute-done
  72.1 1.7 %collective-permute-start = (f32[2,2,4,256]{3,2,1,0:T(4,128)S(1)}, f32[2,2,4,256]{3,2,1,0:T(4,128)S(1)}, u32[]{:S(2)}, u32[]{:S(2)}) collective-permute-start(f32[2,2,4,256]{3,2,1,0:T(4,128)S(1)} %get-tuple-element.404), channel_id=1, source_target_pairs={{1,0},{0,1},{3,2},{2,3},{5,4},{4,5},{7,6},{6,7},{9,8},{8,9},{11,10... | collective-permute-start | bytes 49160 | tf_op jit(solution)/shard_map/while/body/eval_jaxpr/ppermute | solution.py:28
  74.3 1.5 collective-permute-done
  75.9 1.7 %collective-permute-done.1 = f32[2,2,4,256]{3,2,1,0:T(4,128)S(1)} collective-permute-done((f32[2,2,4,256]{3,2,1,0:T(4,128)S(1)}, f32[2,2,4,256]{3,2,1,0:T(4,128)S(1)}, u32[]{:S(2)}, u32[]{:S(2)}) %collective-permute-start.1) | collective-permute-done | bytes 16416 | tf_op jit(solution)/shard_map/while/body/eval_jaxpr/ppermute | solution.py:27
  80.2 1.7 %collective-permute-start.1 = (f32[2,2,4,256]{3,2,1,0:T(4,128)S(1)}, f32[2,2,4,256]{3,2,1,0:T(4,128)S(1)}, u32[]{:S(2)}, u32[]{:S(2)}) collective-permute-start(f32[2,2,4,256]{3,2,1,0:T(4,128)S(1)} %get-tuple-element.405), channel_id=1, source_target_pairs={{0,1},{1,0},{2,3},{3,2},{4,5},{5,4},{6,7},{7,6},{8,9},{9,8},{10,11... | collective-permute-start | bytes 49160 | tf_op jit(solution)/shard_map/while/body/eval_jaxpr/ppermute | solution.py:27
  82.0 1.5 collective-permute-done
  86.1 1.7 %collective-permute-start = (f32[2,2,4,256]{3,2,1,0:T(4,128)S(1)}, f32[2,2,4,256]{3,2,1,0:T(4,128)S(1)}, u32[]{:S(2)}, u32[]{:S(2)}) collective-permute-start(f32[2,2,4,256]{3,2,1,0:T(4,128)S(1)} %get-tuple-element.404), channel_id=1, source_target_pairs={{1,0},{0,1},{3,2},{2,3},{5,4},{4,5},{7,6},{6,7},{9,8},{8,9},{11,10... | collective-permute-start | bytes 49160 | tf_op jit(solution)/shard_map/while/body/eval_jaxpr/ppermute | solution.py:28
  88.4 1.5 collective-permute-done
  89.9 1.7 %collective-permute-done.1 = f32[2,2,4,256]{3,2,1,0:T(4,128)S(1)} collective-permute-done((f32[2,2,4,256]{3,2,1,0:T(4,128)S(1)}, f32[2,2,4,256]{3,2,1,0:T(4,128)S(1)}, u32[]{:S(2)}, u32[]{:S(2)}) %collective-permute-start.1) | collective-permute-done | bytes 16416 | tf_op jit(solution)/shard_map/while/body/eval_jaxpr/ppermute | solution.py:27
  94.3 1.7 %collective-permute-start.1 = (f32[2,2,4,256]{3,2,1,0:T(4,128)S(1)}, f32[2,2,4,256]{3,2,1,0:T(4,128)S(1)}, u32[]{:S(2)}, u32[]{:S(2)}) collective-permute-start(f32[2,2,4,256]{3,2,1,0:T(4,128)S(1)} %get-tuple-element.405), channel_id=1, source_target_pairs={{0,1},{1,0},{2,3},{3,2},{4,5},{5,4},{6,7},{7,6},{8,9},{9,8},{10,11... | collective-permute-start | bytes 49160 | tf_op jit(solution)/shard_map/while/body/eval_jaxpr/ppermute | solution.py:27
  96.1 1.5 collective-permute-done
  100.2 1.7 %collective-permute-start = (f32[2,2,4,256]{3,2,1,0:T(4,128)S(1)}, f32[2,2,4,256]{3,2,1,0:T(4,128)S(1)}, u32[]{:S(2)}, u32[]{:S(2)}) collective-permute-start(f32[2,2,4,256]{3,2,1,0:T(4,128)S(1)} %get-tuple-element.404), channel_id=1, source_target_pairs={{1,0},{0,1},{3,2},{2,3},{5,4},{4,5},{7,6},{6,7},{9,8},{8,9},{11,10... | collective-permute-start | bytes 49160 | tf_op jit(solution)/shard_map/while/body/eval_jaxpr/ppermute | solution.py:28
  102.5 1.5 collective-permute-done
  104.0 1.7 %collective-permute-done.1 = f32[2,2,4,256]{3,2,1,0:T(4,128)S(1)} collective-permute-done((f32[2,2,4,256]{3,2,1,0:T(4,128)S(1)}, f32[2,2,4,256]{3,2,1,0:T(4,128)S(1)}, u32[]{:S(2)}, u32[]{:S(2)}) %collective-permute-start.1) | collective-permute-done | bytes 16416 | tf_op jit(solution)/shard_map/while/body/eval_jaxpr/ppermute | solution.py:27
  108.1 12.7 %all_to_all.63 = f32[2,128,256]{2,0,1:T(2,128)S(1)} all-to-all(f32[2,128,256]{2,0,1:T(2,128)S(1)} %copy.48), channel_id=1, replica_groups=mesh['tm'=16,'band'=2] {'tm'}, dimensions={1} | all-to-all | bytes 524288 | tf_op jit(solution)/shard_map/all_to_all | solution.py:157
  121.0 0.4 fusion.92
  121.6 12.7 %all_to_all.64 = f32[32,8,256]{2,1,0:T(8,128)S(1)} all-to-all(f32[32,8,256]{2,1,0:T(8,128)S(1)} %copy.50), channel_id=1, replica_groups=mesh['tm'=16,'band'=2] {'tm'}, dimensions={0} | all-to-all | bytes 524288 | tf_op jit(solution)/shard_map/all_to_all | solution.py:158
  135.9 1.7 %collective-permute-start.12 = (f32[2,1,256]{2,1,0:T(1,128)S(1)}, f32[2,1,256]{2,1,0:T(1,128)S(1)}, u32[]{:S(2)}, u32[]{:S(2)}) collective-permute-start(f32[2,1,256]{2,1,0:T(1,128)S(1)} %get-tuple-element.266), channel_id=1, source_target_pairs={{1,0},{0,1},{3,2},{2,3},{5,4},{4,5},{7,6},{6,7},{9,8},{8,9},{11,10... | collective-permute-start | bytes 6152 | tf_op jit(solution)/shard_map/ppermute | solution.py:28
  137.5 1.6 collective-permute-done.11
  139.6 7.2 %collective-permute-done.13 = f32[1,128,256]{2,1,0:T(8,128)S(1)} collective-permute-done((f32[1,128,256]{2,1,0:T(8,128)S(1)}, f32[1,128,256]{2,1,0:T(8,128)S(1)}, u32[]{:S(2)}, u32[]{:S(2)}) %collective-permute-start.13) | collective-permute-done | bytes 131104 | tf_op jit(solution)/shard_map/ppermute | solution.py:35
  147.0 2.5 %collective-permute-done.14 = f32[1,128,256]{2,1,0:T(8,128)S(1)} collective-permute-done((f32[1,128,256]{2,1,0:T(8,128)S(1)}, f32[1,128,256]{2,1,0:T(8,128)S(1)}, u32[]{:S(2)}, u32[]{:S(2)}) %collective-permute-start.14) | collective-permute-done | bytes 131104 | tf_op jit(solution)/shard_map/ppermute | solution.py:35
  149.5 1.7 %collective-permute-start.15 = (f32[2,1,256]{2,1,0:T(1,128)S(1)}, f32[2,1,256]{2,1,0:T(1,128)S(1)}, u32[]{:S(2)}, u32[]{:S(2)}) collective-permute-start(f32[2,1,256]{2,1,0:T(1,128)S(1)} %get-tuple-element.259), channel_id=1, source_target_pairs={{0,1},{1,0},{2,3},{3,2},{4,5},{5,4},{6,7},{7,6},{8,9},{9,8},{10,11... | collective-permute-start | bytes 6152 | tf_op jit(solution)/shard_map/ppermute | solution.py:27
  151.6 1.6 collective-permute-done.15
  153.1 1.7 %collective-permute-done.16 = f32[2,1,256]{2,1,0:T(1,128)S(1)} collective-permute-done((f32[2,1,256]{2,1,0:T(1,128)S(1)}, f32[2,1,256]{2,1,0:T(1,128)S(1)}, u32[]{:S(2)}, u32[]{:S(2)}) %collective-permute-start.16) | collective-permute-done | bytes 2080 | tf_op jit(solution)/shard_map/ppermute | solution.py:28
  155.8 0.8 copy-done.5
  156.6 0.9 fusion.35
  (229 shorter events, 25.2 us)
Async XLA Ops:
  1.3 8.5 %copy-start.3 = (s32[2,128,256]{2,1,0:T(8,128)S(1)}, s32[2,128,256]{2,1,0:T(8,128)}, u32[]{:S(2)}) copy-start(s32[2,128,256]{2,1,0:T(8,128)} %param.11) | copy-start | bytes 786436
  1.3 9.1 %collective-permute-start.2 = (s32[1,256]{1,0:T(1,128)S(1)}, s32[1,256]{1,0:T(1,128)S(1)}, u32[]{:S(2)}, u32[]{:S(2)}) collective-permute-start(s32[1,256]{1,0:T(1,128)S(1)} %slice_bitcast_fusion.4), channel_id=1, source_target_pairs={{0,1},{1,0},{2,3},{3,2},{4,5},{5,4},{6,7},{7,6},{8,9},{9,8},{10,11... | collective-permute-start | bytes 3080 | tf_op jit(solution)/shard_map/ppermute | solution.py:35
  5.3 7.2 %collective-permute-start.3 = (f32[1,128,256]{2,1,0:T(8,128)S(1)}, f32[1,128,256]{2,1,0:T(8,128)S(1)}, u32[]{:S(2)}, u32[]{:S(2)}) collective-permute-start(f32[1,128,256]{2,1,0:T(8,128)S(1)} %get-tuple-element.313), channel_id=1, source_target_pairs={{0,2},{2,4},{4,6},{6,8},{8,10},{10,12},{12,14},{14,16},{16,18},{18... | collective-permute-start | bytes 393224 | tf_op jit(solution)/shard_map/ppermute | solution.py:27
  5.4 7.2 %collective-permute-start.4 = (f32[1,128,256]{2,1,0:T(8,128)S(1)}, f32[1,128,256]{2,1,0:T(8,128)S(1)}, u32[]{:S(2)}, u32[]{:S(2)}) collective-permute-start(f32[1,128,256]{2,1,0:T(8,128)S(1)} %get-tuple-element.314), channel_id=1, source_target_pairs={{2,0},{4,2},{6,4},{8,6},{10,8},{12,10},{14,12},{16,14},{18,16},{20... | collective-permute-start | bytes 393224 | tf_op jit(solution)/shard_map/ppermute | solution.py:28
  10.4 2.1 %copy-start = (f32[2,128,256]{2,1,0:T(8,128)S(1)}, f32[2,128,256]{2,1,0:T(8,128)}, u32[]{:S(2)}) copy-start(f32[2,128,256]{2,1,0:T(8,128)} %param.7) | copy-start | bytes 786436
  10.5 2.1 %copy-start.1 = (f32[2,128,256]{2,1,0:T(8,128)S(1)}, f32[2,128,256]{2,1,0:T(8,128)}, u32[]{:S(2)}) copy-start(f32[2,128,256]{2,1,0:T(8,128)} %param.10) | copy-start | bytes 786436
  13.6 3.7 %collective-permute-start.5 = (f32[2,1,256]{2,1,0:T(1,128)S(1)}, f32[2,1,256]{2,1,0:T(1,128)S(1)}, u32[]{:S(2)}, u32[]{:S(2)}) collective-permute-start(f32[2,1,256]{2,1,0:T(1,128)S(1)} %get-tuple-element.297), channel_id=1, source_target_pairs={{0,1},{1,0},{2,3},{3,2},{4,5},{5,4},{6,7},{7,6},{8,9},{9,8},{10,11... | collective-permute-start | bytes 6152 | tf_op jit(solution)/shard_map/ppermute | solution.py:27
  13.7 3.6 %collective-permute-start.6 = (f32[2,1,256]{2,1,0:T(1,128)S(1)}, f32[2,1,256]{2,1,0:T(1,128)S(1)}, u32[]{:S(2)}, u32[]{:S(2)}) collective-permute-start(f32[2,1,256]{2,1,0:T(1,128)S(1)} %get-tuple-element.298), channel_id=1, source_target_pairs={{1,0},{0,1},{3,2},{2,3},{5,4},{4,5},{7,6},{6,7},{9,8},{8,9},{11,10... | collective-permute-start | bytes 6152 | tf_op jit(solution)/shard_map/ppermute | solution.py:28
  17.4 7.2 %collective-permute-start.7 = (f32[1,128,256]{2,1,0:T(8,128)S(1)}, f32[1,128,256]{2,1,0:T(8,128)S(1)}, u32[]{:S(2)}, u32[]{:S(2)}) collective-permute-start(f32[1,128,256]{2,1,0:T(8,128)S(1)} %get-tuple-element.295), channel_id=1, source_target_pairs={{0,2},{2,4},{4,6},{6,8},{8,10},{10,12},{12,14},{14,16},{16,18},{18... | collective-permute-start | bytes 393224 | tf_op jit(solution)/shard_map/ppermute | solution.py:35
  24.7 2.6 %collective-permute-start.8 = (f32[1,128,256]{2,1,0:T(8,128)S(1)}, f32[1,128,256]{2,1,0:T(8,128)S(1)}, u32[]{:S(2)}, u32[]{:S(2)}) collective-permute-start(f32[1,128,256]{2,1,0:T(8,128)S(1)} %get-tuple-element.294), channel_id=1, source_target_pairs={{0,30},{2,0},{4,2},{6,4},{8,6},{10,8},{12,10},{14,12},{16,14},{18,... | collective-permute-start | bytes 393224 | tf_op jit(solution)/shard_map/ppermute | solution.py:35
  27.3 3.7 %collective-permute-start.9 = (f32[2,1,256]{2,1,0:T(1,128)S(1)}, f32[2,1,256]{2,1,0:T(1,128)S(1)}, u32[]{:S(2)}, u32[]{:S(2)}) collective-permute-start(f32[2,1,256]{2,1,0:T(1,128)S(1)} %get-tuple-element.291), channel_id=1, source_target_pairs={{0,1},{1,0},{2,3},{3,2},{4,5},{5,4},{6,7},{7,6},{8,9},{9,8},{10,11... | collective-permute-start | bytes 6152 | tf_op jit(solution)/shard_map/ppermute | solution.py:27
  29.4 3.6 %collective-permute-start.10 = (f32[2,1,256]{2,1,0:T(1,128)S(1)}, f32[2,1,256]{2,1,0:T(1,128)S(1)}, u32[]{:S(2)}, u32[]{:S(2)}) collective-permute-start(f32[2,1,256]{2,1,0:T(1,128)S(1)} %get-tuple-element.292), channel_id=1, source_target_pairs={{1,0},{0,1},{3,2},{2,3},{5,4},{4,5},{7,6},{6,7},{9,8},{8,9},{11,10... | collective-permute-start | bytes 6152 | tf_op jit(solution)/shard_map/ppermute | solution.py:28
  33.8 1.0 copy-start.4
  35.9 14.5 %all-to-all-start = ((f32[2,128,256]{2,0,1:T(2,128)}), f32[2,128,256]{2,0,1:T(2,128)S(1)}, u32[]{:S(2)}, u32[]{:S(2)}) async-start(f32[2,128,256]{2,0,1:T(2,128)} %copy.43), calls=%async_computation | async-start | bytes 524288 | tf_op jit(solution)/shard_map/all_to_all | solution.py:128
  52.0 13.5 %all-to-all-start.1 = ((f32[32,8,256]{2,1,0:T(8,128)}), f32[32,8,256]{2,1,0:T(8,128)S(1)}, u32[]{:S(2)}, u32[]{:S(2)}) async-start(f32[32,8,256]{2,1,0:T(8,128)} %copy.46), calls=%async_computation.1 | async-start | bytes 524288 | tf_op jit(solution)/shard_map/all_to_all | solution.py:129
  65.7 3.8 %collective-permute-start = (f32[2,2,4,256]{3,2,1,0:T(4,128)S(1)}, f32[2,2,4,256]{3,2,1,0:T(4,128)S(1)}, u32[]{:S(2)}, u32[]{:S(2)}) collective-permute-start(f32[2,2,4,256]{3,2,1,0:T(4,128)S(1)} %get-tuple-element.404), channel_id=1, source_target_pairs={{1,0},{0,1},{3,2},{2,3},{5,4},{4,5},{7,6},{6,7},{9,8},{8,9},{11,10... | collective-permute-start | bytes 49160 | tf_op jit(solution)/shard_map/while/body/eval_jaxpr/ppermute | solution.py:28
  66.1 3.7 %collective-permute-start.1 = (f32[2,2,4,256]{3,2,1,0:T(4,128)S(1)}, f32[2,2,4,256]{3,2,1,0:T(4,128)S(1)}, u32[]{:S(2)}, u32[]{:S(2)}) collective-permute-start(f32[2,2,4,256]{3,2,1,0:T(4,128)S(1)} %get-tuple-element.405), channel_id=1, source_target_pairs={{0,1},{1,0},{2,3},{3,2},{4,5},{5,4},{6,7},{7,6},{8,9},{9,8},{10,11... | collective-permute-start | bytes 49160 | tf_op jit(solution)/shard_map/while/body/eval_jaxpr/ppermute | solution.py:27
  72.1 3.8 %collective-permute-start = (f32[2,2,4,256]{3,2,1,0:T(4,128)S(1)}, f32[2,2,4,256]{3,2,1,0:T(4,128)S(1)}, u32[]{:S(2)}, u32[]{:S(2)}) collective-permute-start(f32[2,2,4,256]{3,2,1,0:T(4,128)S(1)} %get-tuple-element.404), channel_id=1, source_target_pairs={{1,0},{0,1},{3,2},{2,3},{5,4},{4,5},{7,6},{6,7},{9,8},{8,9},{11,10... | collective-permute-start | bytes 49160 | tf_op jit(solution)/shard_map/while/body/eval_jaxpr/ppermute | solution.py:28
  73.8 3.7 %collective-permute-start.1 = (f32[2,2,4,256]{3,2,1,0:T(4,128)S(1)}, f32[2,2,4,256]{3,2,1,0:T(4,128)S(1)}, u32[]{:S(2)}, u32[]{:S(2)}) collective-permute-start(f32[2,2,4,256]{3,2,1,0:T(4,128)S(1)} %get-tuple-element.405), channel_id=1, source_target_pairs={{0,1},{1,0},{2,3},{3,2},{4,5},{5,4},{6,7},{7,6},{8,9},{9,8},{10,11... | collective-permute-start | bytes 49160 | tf_op jit(solution)/shard_map/while/body/eval_jaxpr/ppermute | solution.py:27
  79.8 3.8 %collective-permute-start = (f32[2,2,4,256]{3,2,1,0:T(4,128)S(1)}, f32[2,2,4,256]{3,2,1,0:T(4,128)S(1)}, u32[]{:S(2)}, u32[]{:S(2)}) collective-permute-start(f32[2,2,4,256]{3,2,1,0:T(4,128)S(1)} %get-tuple-element.404), channel_id=1, source_target_pairs={{1,0},{0,1},{3,2},{2,3},{5,4},{4,5},{7,6},{6,7},{9,8},{8,9},{11,10... | collective-permute-start | bytes 49160 | tf_op jit(solution)/shard_map/while/body/eval_jaxpr/ppermute | solution.py:28
  80.2 3.7 %collective-permute-start.1 = (f32[2,2,4,256]{3,2,1,0:T(4,128)S(1)}, f32[2,2,4,256]{3,2,1,0:T(4,128)S(1)}, u32[]{:S(2)}, u32[]{:S(2)}) collective-permute-start(f32[2,2,4,256]{3,2,1,0:T(4,128)S(1)} %get-tuple-element.405), channel_id=1, source_target_pairs={{0,1},{1,0},{2,3},{3,2},{4,5},{5,4},{6,7},{7,6},{8,9},{9,8},{10,11... | collective-permute-start | bytes 49160 | tf_op jit(solution)/shard_map/while/body/eval_jaxpr/ppermute | solution.py:27
  86.1 3.8 %collective-permute-start = (f32[2,2,4,256]{3,2,1,0:T(4,128)S(1)}, f32[2,2,4,256]{3,2,1,0:T(4,128)S(1)}, u32[]{:S(2)}, u32[]{:S(2)}) collective-permute-start(f32[2,2,4,256]{3,2,1,0:T(4,128)S(1)} %get-tuple-element.404), channel_id=1, source_target_pairs={{1,0},{0,1},{3,2},{2,3},{5,4},{4,5},{7,6},{6,7},{9,8},{8,9},{11,10... | collective-permute-start | bytes 49160 | tf_op jit(solution)/shard_map/while/body/eval_jaxpr/ppermute | solution.py:28
  87.9 3.7 %collective-permute-start.1 = (f32[2,2,4,256]{3,2,1,0:T(4,128)S(1)}, f32[2,2,4,256]{3,2,1,0:T(4,128)S(1)}, u32[]{:S(2)}, u32[]{:S(2)}) collective-permute-start(f32[2,2,4,256]{3,2,1,0:T(4,128)S(1)} %get-tuple-element.405), channel_id=1, source_target_pairs={{0,1},{1,0},{2,3},{3,2},{4,5},{5,4},{6,7},{7,6},{8,9},{9,8},{10,11... | collective-permute-start | bytes 49160 | tf_op jit(solution)/shard_map/while/body/eval_jaxpr/ppermute | solution.py:27
  93.8 3.8 %collective-permute-start = (f32[2,2,4,256]{3,2,1,0:T(4,128)S(1)}, f32[2,2,4,256]{3,2,1,0:T(4,128)S(1)}, u32[]{:S(2)}, u32[]{:S(2)}) collective-permute-start(f32[2,2,4,256]{3,2,1,0:T(4,128)S(1)} %get-tuple-element.404), channel_id=1, source_target_pairs={{1,0},{0,1},{3,2},{2,3},{5,4},{4,5},{7,6},{6,7},{9,8},{8,9},{11,10... | collective-permute-start | bytes 49160 | tf_op jit(solution)/shard_map/while/body/eval_jaxpr/ppermute | solution.py:28
  94.3 3.7 %collective-permute-start.1 = (f32[2,2,4,256]{3,2,1,0:T(4,128)S(1)}, f32[2,2,4,256]{3,2,1,0:T(4,128)S(1)}, u32[]{:S(2)}, u32[]{:S(2)}) collective-permute-start(f32[2,2,4,256]{3,2,1,0:T(4,128)S(1)} %get-tuple-element.405), channel_id=1, source_target_pairs={{0,1},{1,0},{2,3},{3,2},{4,5},{5,4},{6,7},{7,6},{8,9},{9,8},{10,11... | collective-permute-start | bytes 49160 | tf_op jit(solution)/shard_map/while/body/eval_jaxpr/ppermute | solution.py:27
  100.2 3.8 %collective-permute-start = (f32[2,2,4,256]{3,2,1,0:T(4,128)S(1)}, f32[2,2,4,256]{3,2,1,0:T(4,128)S(1)}, u32[]{:S(2)}, u32[]{:S(2)}) collective-permute-start(f32[2,2,4,256]{3,2,1,0:T(4,128)S(1)} %get-tuple-element.404), channel_id=1, source_target_pairs={{1,0},{0,1},{3,2},{2,3},{5,4},{4,5},{7,6},{6,7},{9,8},{8,9},{11,10... | collective-permute-start | bytes 49160 | tf_op jit(solution)/shard_map/while/body/eval_jaxpr/ppermute | solution.py:28
  101.9 3.7 %collective-permute-start.1 = (f32[2,2,4,256]{3,2,1,0:T(4,128)S(1)}, f32[2,2,4,256]{3,2,1,0:T(4,128)S(1)}, u32[]{:S(2)}, u32[]{:S(2)}) collective-permute-start(f32[2,2,4,256]{3,2,1,0:T(4,128)S(1)} %get-tuple-element.405), channel_id=1, source_target_pairs={{0,1},{1,0},{2,3},{3,2},{4,5},{5,4},{6,7},{7,6},{8,9},{9,8},{10,11... | collective-permute-start | bytes 49160 | tf_op jit(solution)/shard_map/while/body/eval_jaxpr/ppermute | solution.py:27
  134.4 21.3 %copy-start.2 = (f32[2,128,256]{2,1,0:T(8,128)}, f32[2,128,256]{2,1,0:T(8,128)S(1)}, u32[]{:S(2)}) copy-start(f32[2,128,256]{2,1,0:T(8,128)S(1)} %get-tuple-element.207) | copy-start | bytes 786436
  135.4 3.7 %collective-permute-start.11 = (f32[2,1,256]{2,1,0:T(1,128)S(1)}, f32[2,1,256]{2,1,0:T(1,128)S(1)}, u32[]{:S(2)}, u32[]{:S(2)}) collective-permute-start(f32[2,1,256]{2,1,0:T(1,128)S(1)} %get-tuple-element.265), channel_id=1, source_target_pairs={{0,1},{1,0},{2,3},{3,2},{4,5},{5,4},{6,7},{7,6},{8,9},{9,8},{10,11... | collective-permute-start | bytes 6152 | tf_op jit(solution)/shard_map/ppermute | solution.py:27
  135.9 3.6 %collective-permute-start.12 = (f32[2,1,256]{2,1,0:T(1,128)S(1)}, f32[2,1,256]{2,1,0:T(1,128)S(1)}, u32[]{:S(2)}, u32[]{:S(2)}) collective-permute-start(f32[2,1,256]{2,1,0:T(1,128)S(1)} %get-tuple-element.266), channel_id=1, source_target_pairs={{1,0},{0,1},{3,2},{2,3},{5,4},{4,5},{7,6},{6,7},{9,8},{8,9},{11,10... | collective-permute-start | bytes 6152 | tf_op jit(solution)/shard_map/ppermute | solution.py:28
  139.6 7.2 %collective-permute-start.13 = (f32[1,128,256]{2,1,0:T(8,128)S(1)}, f32[1,128,256]{2,1,0:T(8,128)S(1)}, u32[]{:S(2)}, u32[]{:S(2)}) collective-permute-start(f32[1,128,256]{2,1,0:T(8,128)S(1)} %get-tuple-element.263), channel_id=1, source_target_pairs={{0,2},{2,4},{4,6},{6,8},{8,10},{10,12},{12,14},{14,16},{16,18},{18... | collective-permute-start | bytes 393224 | tf_op jit(solution)/shard_map/ppermute | solution.py:35
  146.9 2.6 %collective-permute-start.14 = (f32[1,128,256]{2,1,0:T(8,128)S(1)}, f32[1,128,256]{2,1,0:T(8,128)S(1)}, u32[]{:S(2)}, u32[]{:S(2)}) collective-permute-start(f32[1,128,256]{2,1,0:T(8,128)S(1)} %get-tuple-element.262), channel_id=1, source_target_pairs={{0,30},{2,0},{4,2},{6,4},{8,6},{10,8},{12,10},{14,12},{16,14},{18,... | collective-permute-start | bytes 393224 | tf_op jit(solution)/shard_map/ppermute | solution.py:35
  149.5 3.7 %collective-permute-start.15 = (f32[2,1,256]{2,1,0:T(1,128)S(1)}, f32[2,1,256]{2,1,0:T(1,128)S(1)}, u32[]{:S(2)}, u32[]{:S(2)}) collective-permute-start(f32[2,1,256]{2,1,0:T(1,128)S(1)} %get-tuple-element.259), channel_id=1, source_target_pairs={{0,1},{1,0},{2,3},{3,2},{4,5},{5,4},{6,7},{7,6},{8,9},{9,8},{10,11... | collective-permute-start | bytes 6152 | tf_op jit(solution)/shard_map/ppermute | solution.py:27
  151.2 3.6 %collective-permute-start.16 = (f32[2,1,256]{2,1,0:T(1,128)S(1)}, f32[2,1,256]{2,1,0:T(1,128)S(1)}, u32[]{:S(2)}, u32[]{:S(2)}) collective-permute-start(f32[2,1,256]{2,1,0:T(1,128)S(1)} %get-tuple-element.260), channel_id=1, source_target_pairs={{1,0},{0,1},{3,2},{2,3},{5,4},{4,5},{7,6},{6,7},{9,8},{8,9},{11,10... | collective-permute-start | bytes 6152 | tf_op jit(solution)/shard_map/ppermute | solution.py:28
  155.6 1.0 copy-start.5
where the time goes:
time: 158 us
  waiting for transfers between devices  66.5 us (42%)
  starting transfers between devices  36.7 us (23%)
  blocking collectives  25.4 us (16%)
  local copies, waits for them, and re-layouts  14.2 us (9%)
  other arithmetic  11.9 us (8%)
    ppermute x5, waiting for transfers between devices, passed_along(): lax.ppermute(value, axis, [(i, (i + by) % size) for i in range(size)])  19.3 us
    ppermute x11, starting transfers between devices, extended(): after = lax.ppermute(leading, axis, down)  15 us
    ppermute x11, waiting for transfers between devices, extended(): before = lax.ppermute(last, axis, up)  13.9 us
    ppermute x11, waiting for transfers between devices, extended(): after = lax.ppermute(leading, axis, down)  13.4 us
    all_to_all x1, blocking collectives, shards(): lax.all_to_all(accum, 'tm', split_axis=1, concat_axis=0, tiled=True)  12.7 us
    all_to_all x1, blocking collectives, shards(): lax.all_to_all(mixed_back, 'tm', split_axis=0, concat_axis=1, tiled=True)  12.7 us
    ppermute x11, starting transfers between devices, extended(): before = lax.ppermute(last, axis, up)  10.4 us
    all_to_all x1, waiting for transfers between devices, shards(): lax.all_to_all(residual, 'tm', split_axis=1, concat_axis=0, tiled=True)  9.98 us
  transfers between devices with their start and end apart: 29, of which 27 were waited for; matrix products, arithmetic and copies ran while one was open for 2% of the time, Pallas kernels for 0%

commit v1 on v0

--- a/solution.py
+++ b/solution.py
@@ -1,3 +1,4 @@
+import functools
 import math
 import jax
 import jax.numpy as jnp
@@ -15,6 +16,27 @@
 cheb_slope = 0.5
 half_width = 4.0
 deep_width = 4
+
+
+def enter_case(slab_in, axis_id):
+    long_array, w1 = (lax.axis_size(axis_id), lax.axis_index(axis_id))
+    b_now = slab_in.shape[1] // long_array
+    aux = list(slab_in.shape)
+    aux[1] = b_now
+    mid_arr = aux[0]
+    aux[0] = mid_arr * long_array
+    left_arr = jnp.zeros(aux, slab_in.dtype)
+    for t in range(long_array):
+        next_value = lax.dynamic_slice_in_dim(slab_in, (w1 ^ t) * b_now, b_now, axis=1)
+        if t:
+            next_value = lax.ppermute(
+                next_value, axis_id, tuple(((hop_no, hop_no ^ t) for hop_no in range(long_array)))
+            )
+        left_arr = lax.dynamic_update_slice_in_dim(left_arr, next_value, (w1 ^ t) * mid_arr, axis=0)
+    return left_arr
+
+
+produce_zones_in = functools.partial(enter_case, axis_id="tm")
 
 
 def extended(value, sides, width):
@@ -154,7 +176,7 @@
         return (accum, rem_wide, dir_wide, weight_now)
 
     accum = lax.fori_loop(0, ORDER // deep_width, sweep_block, start)[0]
-    mixed_back = to_slices(lax.all_to_all(accum, "tm", split_axis=1, concat_axis=0, tiled=True))
+    mixed_back = to_slices(produce_zones_in(accum))
     timed = lax.all_to_all(mixed_back, "tm", split_axis=0, concat_axis=1, tiled=True)
     solution = guess + relaxation * timed
     propagated = apply_pairs(expo * solution, (0, 1, 2, 3))

time: 158 us -> 171 us (1.082)
  starting transfers between devices: 36.7 us -> 58 us
  blocking collectives: 25.4 us -> 14.4 us
  waiting for transfers between devices: 66.5 us -> 68.4 us
    ppermute x0 -> x15, starting transfers between devices: none -> 21.1 us  [enter_case(): lax.ppermute(next_value, axis_id, tuple(((hop_no, hop_no ^ t) for hop_no...]
    all_to_all x1 -> x0, blocking collectives: 12.7 us -> none  [shards(): lax.all_to_all(accum, 'tm', split_axis=1, concat_axis=0, tiled=True)]
    ppermute x11, waiting for transfers between devices: 13.9 us -> 10.9 us  [extended(): before = lax.ppermute(last, axis, up)]
    ppermute x0 -> x15, waiting for transfers between devices: none -> 2.76 us  [enter_case(): lax.ppermute(next_value, axis_id, tuple(((hop_no, hop_no ^ t) for hop_no...]
    ppermute x11, starting transfers between devices: 10.4 us -> 12.6 us  [extended(): before = lax.ppermute(last, axis, up)]
    all_to_all x1, blocking collectives: 12.7 us -> 14.4 us  [shards(): lax.all_to_all(mixed_back, 'tm', split_axis=0, concat_axis=1, tiled=True)]
  transfers between devices with their start and end apart: 29 -> 44, of which waited for: 27 -> 29; matrix products, arithmetic and copies ran while one was open for 2% -> 1% of each run, Pallas kernels for 0% -> 0%
where the time goes in v1:
time: 171 us; the launch traced here: 170 us
  waiting for transfers between devices  68.4 us (40%)
  starting transfers between devices  58 us (34%)
  blocking collectives  14.4 us (8%)
  local copies, waits for them, and re-layouts  14.2 us (8%)
  other arithmetic  11.9 us (7%)
    ppermute x15, starting transfers between devices, enter_case(): lax.ppermute(next_value, axis_id, tuple(((hop_no, hop_no ^ t) for hop_no...  21.1 us
    ppermute x5, waiting for transfers between devices, passed_along(): lax.ppermute(value, axis, [(i, (i + by) % size) for i in range(size)])  20.4 us
    ppermute x11, waiting for transfers between devices, extended(): after = lax.ppermute(leading, axis, down)  14.7 us
    all_to_all x1, blocking collectives, shards(): lax.all_to_all(mixed_back, 'tm', split_axis=0, concat_axis=1, tiled=True)  14.4 us
    ppermute x11, starting transfers between devices, extended(): after = lax.ppermute(leading, axis, down)  13.9 us
    ppermute x11, starting transfers between devices, extended(): before = lax.ppermute(last, axis, up)  12.6 us
    ppermute x11, waiting for transfers between devices, extended(): before = lax.ppermute(last, axis, up)  10.9 us
    all_to_all x1, waiting for transfers between devices, shards(): lax.all_to_all(residual, 'tm', split_axis=1, concat_axis=0, tiled=True)  9.98 us
  transfers between devices with their start and end apart: 44, of which 29 were waited for; matrix products, arithmetic and copies ran while one was open for 1% of the time, Pallas kernels for 0%

profile of v1, /device:TPU:0, one launch (start us, length us, event | category | flops | bytes accessed | tf_op | source)
XLA Modules:
  0.0 170.2 jit_solution(246182008078574686)
XLA Ops:
  2.2 5.0 %collective-permute-start.4 = (f32[1,128,256]{2,1,0:T(8,128)S(1)}, f32[1,128,256]{2,1,0:T(8,128)S(1)}, u32[]{:S(2)}, u32[]{:S(2)}) collective-permute-start(f32[1,128,256]{2,1,0:T(8,128)S(1)} %get-tuple-element.330), channel_id=1, source_target_pairs={{2,0},{4,2},{6,4},{8,6},{10,8},{12,10},{14,12},{16,14},{18,16},{20... | collective-permute-start | bytes 393224 | tf_op jit(solution)/shard_map/ppermute | solution.py:50
  7.3 1.9 %collective-permute-start.2 = (s32[1,256]{1,0:T(1,128)S(1)}, s32[1,256]{1,0:T(1,128)S(1)}, u32[]{:S(2)}, u32[]{:S(2)}) collective-permute-start(s32[1,256]{1,0:T(1,128)S(1)} %slice_bitcast_fusion.4), channel_id=1, source_target_pairs={{0,1},{1,0},{2,3},{3,2},{4,5},{5,4},{6,7},{7,6},{8,9},{9,8},{10,11... | collective-permute-start | bytes 3080 | tf_op jit(solution)/shard_map/ppermute | solution.py:57
  9.8 1.1 collective-permute-done.2
  12.9 1.9 %collective-permute-start.5 = (f32[2,1,256]{2,1,0:T(1,128)S(1)}, f32[2,1,256]{2,1,0:T(1,128)S(1)}, u32[]{:S(2)}, u32[]{:S(2)}) collective-permute-start(f32[2,1,256]{2,1,0:T(1,128)S(1)} %get-tuple-element.313), channel_id=1, source_target_pairs={{0,1},{1,0},{2,3},{3,2},{4,5},{5,4},{6,7},{7,6},{8,9},{9,8},{10,11... | collective-permute-start | bytes 6152 | tf_op jit(solution)/shard_map/ppermute | solution.py:49
  15.0 1.6 collective-permute-done.5
  16.6 1.9 %collective-permute-done.6 = f32[2,1,256]{2,1,0:T(1,128)S(1)} collective-permute-done((f32[2,1,256]{2,1,0:T(1,128)S(1)}, f32[2,1,256]{2,1,0:T(1,128)S(1)}, u32[]{:S(2)}, u32[]{:S(2)}) %collective-permute-start.6) | collective-permute-done | bytes 2080 | tf_op jit(solution)/shard_map/ppermute | solution.py:50
  18.6 7.2 %collective-permute-done.7 = f32[1,128,256]{2,1,0:T(8,128)S(1)} collective-permute-done((f32[1,128,256]{2,1,0:T(8,128)S(1)}, f32[1,128,256]{2,1,0:T(8,128)S(1)}, u32[]{:S(2)}, u32[]{:S(2)}) %collective-permute-start.7) | collective-permute-done | bytes 131104 | tf_op jit(solution)/shard_map/ppermute | solution.py:57
  26.0 2.5 %collective-permute-done.8 = f32[1,128,256]{2,1,0:T(8,128)S(1)} collective-permute-done((f32[1,128,256]{2,1,0:T(8,128)S(1)}, f32[1,128,256]{2,1,0:T(8,128)S(1)}, u32[]{:S(2)}, u32[]{:S(2)}) %collective-permute-start.8) | collective-permute-done | bytes 131104 | tf_op jit(solution)/shard_map/ppermute | solution.py:57
  28.7 1.9 %collective-permute-start.9 = (f32[2,1,256]{2,1,0:T(1,128)S(1)}, f32[2,1,256]{2,1,0:T(1,128)S(1)}, u32[]{:S(2)}, u32[]{:S(2)}) collective-permute-start(f32[2,1,256]{2,1,0:T(1,128)S(1)} %get-tuple-element.307), channel_id=1, source_target_pairs={{0,1},{1,0},{2,3},{3,2},{4,5},{5,4},{6,7},{7,6},{8,9},{9,8},{10,11... | collective-permute-start | bytes 6152 | tf_op jit(solution)/shard_map/ppermute | solution.py:49
  30.6 1.6 collective-permute-done.10
  35.3 4.7 %all-to-all-start = ((f32[2,128,256]{2,0,1:T(2,128)}), f32[2,128,256]{2,0,1:T(2,128)S(1)}, u32[]{:S(2)}, u32[]{:S(2)}) async-start(f32[2,128,256]{2,0,1:T(2,128)} %copy.87), calls=%async_computation | async-start | bytes 524288 | tf_op jit(solution)/shard_map/all_to_all | solution.py:150
  40.0 10.0 %all-to-all-done = f32[2,128,256]{2,0,1:T(2,128)S(1)} async-done(((f32[2,128,256]{2,0,1:T(2,128)}), f32[2,128,256]{2,0,1:T(2,128)S(1)}, u32[]{:S(2)}, u32[]{:S(2)}) %all-to-all-start) | async-done | bytes 262176 | tf_op jit(solution)/shard_map/all_to_all | solution.py:150
  51.6 3.5 %all-to-all-start.1 = ((f32[32,8,256]{2,1,0:T(8,128)}), f32[32,8,256]{2,1,0:T(8,128)S(1)}, u32[]{:S(2)}, u32[]{:S(2)}) async-start(f32[32,8,256]{2,1,0:T(8,128)} %copy.90), calls=%async_computation.1 | async-start | bytes 524288 | tf_op jit(solution)/shard_map/all_to_all | solution.py:151
  55.5 9.6 %all-to-all-done.1 = f32[32,8,256]{2,1,0:T(8,128)S(1)} async-done(((f32[32,8,256]{2,1,0:T(8,128)}), f32[32,8,256]{2,1,0:T(8,128)S(1)}, u32[]{:S(2)}, u32[]{:S(2)}) %all-to-all-start.1) | async-done | bytes 262176 | tf_op jit(solution)/shard_map/all_to_all | solution.py:151
  65.2 42.2 %while.22 = (s32[]{:T(128)}, f32[2,128,256]{2,1,0:T(8,128)S(1)}, f32[2,128,256]{2,1,0:T(8,128)S(1)}, f32[2,128,256]{2,1,0:T(8,128)S(1)}, f32[2,1,1]{0,2,1:T(1,12...) while((s32[]{:T(128)}, f32[2,128,256]{2,1,0:T(8,128)S(1)}, ...), condition=%wide.region_1.2_spmd.clone.clone.clone, body=%wide.region_0.1_spmd.clone.clone.clone.sunk | while | flops 3704962 | bytes 17105376 | solution.py:178
  65.3 1.7 %collective-permute-start = (f32[2,2,4,256]{3,2,1,0:T(4,128)S(1)}, f32[2,2,4,256]{3,2,1,0:T(4,128)S(1)}, u32[]{:S(2)}, u32[]{:S(2)}) collective-permute-start(f32[2,2,4,256]{3,2,1,0:T(4,128)S(1)} %get-tuple-element.420), channel_id=1, source_target_pairs={{1,0},{0,1},{3,2},{2,3},{5,4},{4,5},{7,6},{6,7},{9,8},{8,9},{11,10... | collective-permute-start | bytes 49160 | tf_op jit(solution)/shard_map/while/body/eval_jaxpr/ppermute | solution.py:50
  67.5 1.5 collective-permute-done
  69.1 1.7 collective-permute-done.1
  73.4 1.7 collective-permute-start.1
  75.2 1.5 collective-permute-done
  79.3 1.7 %collective-permute-start = (f32[2,2,4,256]{3,2,1,0:T(4,128)S(1)}, f32[2,2,4,256]{3,2,1,0:T(4,128)S(1)}, u32[]{:S(2)}, u32[]{:S(2)}) collective-permute-start(f32[2,2,4,256]{3,2,1,0:T(4,128)S(1)} %get-tuple-element.420), channel_id=1, source_target_pairs={{1,0},{0,1},{3,2},{2,3},{5,4},{4,5},{7,6},{6,7},{9,8},{8,9},{11,10... | collective-permute-start | bytes 49160 | tf_op jit(solution)/shard_map/while/body/eval_jaxpr/ppermute | solution.py:50
  81.6 1.5 collective-permute-done
  83.1 1.7 collective-permute-done.1
  87.4 1.7 collective-permute-start.1
  89.3 1.5 collective-permute-done
  93.4 1.7 %collective-permute-start = (f32[2,2,4,256]{3,2,1,0:T(4,128)S(1)}, f32[2,2,4,256]{3,2,1,0:T(4,128)S(1)}, u32[]{:S(2)}, u32[]{:S(2)}) collective-permute-start(f32[2,2,4,256]{3,2,1,0:T(4,128)S(1)} %get-tuple-element.420), channel_id=1, source_target_pairs={{1,0},{0,1},{3,2},{2,3},{5,4},{4,5},{7,6},{6,7},{9,8},{8,9},{11,10... | collective-permute-start | bytes 49160 | tf_op jit(solution)/shard_map/while/body/eval_jaxpr/ppermute | solution.py:50
  95.7 1.5 collective-permute-done
  97.2 1.7 collective-permute-done.1
  101.5 1.7 collective-permute-start.1
  103.3 1.5 collective-permute-done
  107.7 1.8 %collective-permute-start.13 = (f32[2,8,256]{2,1,0:T(8,128)S(1)}, f32[2,8,256]{2,1,0:T(8,128)S(1)}, u32[]{:S(2)}, u32[]{:S(2)}) collective-permute-start(f32[2,8,256]{2,1,0:T(8,128)S(1)} %get-tuple-element.289), channel_id=1, source_target_pairs={{0,6},{2,4},{4,2},{6,0},{8,14},{10,12},{12,10},{14,8},{16,22},{18,... | collective-permute-start | bytes 49160 | tf_op jit(solution)/shard_map/ppermute | solution.py:32
  109.5 1.7 %collective-permute-start.15 = (f32[2,8,256]{2,1,0:T(8,128)S(1)}, f32[2,8,256]{2,1,0:T(8,128)S(1)}, u32[]{:S(2)}, u32[]{:S(2)}) collective-permute-start(f32[2,8,256]{2,1,0:T(8,128)S(1)} %get-tuple-element.287), channel_id=1, source_target_pairs={{0,10},{2,8},{4,14},{6,12},{8,2},{10,0},{12,6},{14,4},{16,26},{18,... | collective-permute-start | bytes 49160 | tf_op jit(solution)/shard_map/ppermute | solution.py:32
  111.8 2.2 %collective-permute-start.17 = (f32[2,8,256]{2,1,0:T(8,128)S(1)}, f32[2,8,256]{2,1,0:T(8,128)S(1)}, u32[]{:S(2)}, u32[]{:S(2)}) collective-permute-start(f32[2,8,256]{2,1,0:T(8,128)S(1)} %get-tuple-element.285), channel_id=1, source_target_pairs={{0,14},{2,12},{4,10},{6,8},{8,6},{10,4},{12,2},{14,0},{16,30},{18,... | collective-permute-start | bytes 49160 | tf_op jit(solution)/shard_map/ppermute | solution.py:32
  114.1 1.1 collective-permute-start.18
  115.2 1.7 collective-permute-start.19
  117.5 3.1 %collective-permute-start.21 = (f32[2,8,256]{2,1,0:T(8,128)S(1)}, f32[2,8,256]{2,1,0:T(8,128)S(1)}, u32[]{:S(2)}, u32[]{:S(2)}) collective-permute-start(f32[2,8,256]{2,1,0:T(8,128)S(1)} %get-tuple-element.281), channel_id=1, source_target_pairs={{0,22},{2,20},{4,18},{6,16},{8,30},{10,28},{12,26},{14,24},{16,6},... | collective-permute-start | bytes 49160 | tf_op jit(solution)/shard_map/ppermute | solution.py:32
  121.7 2.6 %collective-permute-start.23 = (f32[2,8,256]{2,1,0:T(8,128)S(1)}, f32[2,8,256]{2,1,0:T(8,128)S(1)}, u32[]{:S(2)}, u32[]{:S(2)}) collective-permute-start(f32[2,8,256]{2,1,0:T(8,128)S(1)} %get-tuple-element.294), channel_id=1, source_target_pairs={{0,26},{2,24},{4,30},{6,28},{8,18},{10,16},{12,22},{14,20},{16,10}... | collective-permute-start | bytes 49160 | tf_op jit(solution)/shard_map/ppermute | solution.py:32
  124.4 1.6 collective-permute-start.24
  126.0 3.0 %collective-permute-start.25 = (f32[2,8,256]{2,1,0:T(8,128)S(1)}, f32[2,8,256]{2,1,0:T(8,128)S(1)}, u32[]{:S(2)}, u32[]{:S(2)}) collective-permute-start(f32[2,8,256]{2,1,0:T(8,128)S(1)} %get-tuple-element.279), channel_id=1, source_target_pairs={{0,30},{2,28},{4,26},{6,24},{8,22},{10,20},{12,18},{14,16},{16,14}... | collective-permute-start | bytes 49160 | tf_op jit(solution)/shard_map/ppermute | solution.py:32
  129.2 1.7 %collective-permute-done.24 = f32[2,8,256]{2,1,0:T(8,128)S(1)} collective-permute-done((f32[2,8,256]{2,1,0:T(8,128)S(1)}, f32[2,8,256]{2,1,0:T(8,128)S(1)}, u32[]{:S(2)}, u32[]{:S(2)}) %collective-permute-start.24) | collective-permute-done | bytes 16416 | tf_op jit(solution)/shard_map/ppermute | solution.py:32
  132.5 14.4 %all_to_all.45 = f32[32,8,256]{2,1,0:T(8,128)S(1)} all-to-all(f32[32,8,256]{2,1,0:T(8,128)S(1)} %copy.108), channel_id=1, replica_groups=mesh['tm'=16,'band'=2] {'tm'}, dimensions={0} | all-to-all | bytes 524288 | tf_op jit(solution)/shard_map/all_to_all | solution.py:180
  148.1 1.7 %collective-permute-start.26 = (f32[2,1,256]{2,1,0:T(1,128)S(1)}, f32[2,1,256]{2,1,0:T(1,128)S(1)}, u32[]{:S(2)}, u32[]{:S(2)}) collective-permute-start(f32[2,1,256]{2,1,0:T(1,128)S(1)} %get-tuple-element.265), channel_id=1, source_target_pairs={{0,1},{1,0},{2,3},{3,2},{4,5},{5,4},{6,7},{7,6},{8,9},{9,8},{10,11... | collective-permute-start | bytes 6152 | tf_op jit(solution)/shard_map/ppermute | solution.py:49
  150.2 1.6 collective-permute-done.26
  151.7 1.7 collective-permute-done.27
  153.6 7.2 %collective-permute-done.28 = f32[1,128,256]{2,1,0:T(8,128)S(1)} collective-permute-done((f32[1,128,256]{2,1,0:T(8,128)S(1)}, f32[1,128,256]{2,1,0:T(8,128)S(1)}, u32[]{:S(2)}, u32[]{:S(2)}) %collective-permute-start.28) | collective-permute-done | bytes 131104 | tf_op jit(solution)/shard_map/ppermute | solution.py:57
  160.9 2.5 %collective-permute-done.29 = f32[1,128,256]{2,1,0:T(8,128)S(1)} collective-permute-done((f32[1,128,256]{2,1,0:T(8,128)S(1)}, f32[1,128,256]{2,1,0:T(8,128)S(1)}, u32[]{:S(2)}, u32[]{:S(2)}) %collective-permute-start.29) | collective-permute-done | bytes 131104 | tf_op jit(solution)/shard_map/ppermute | solution.py:57
  163.9 1.7 collective-permute-start.31
  165.5 1.6 collective-permute-done.30
  (273 shorter events, 36.3 us)
Async XLA Ops:
  0.6 6.6 %copy-start.3 = (s32[2,128,256]{2,1,0:T(8,128)S(1)}, s32[2,128,256]{2,1,0:T(8,128)}, u32[]{:S(2)}) copy-start(s32[2,128,256]{2,1,0:T(8,128)} %param.11) | copy-start | bytes 786436
  1.7 9.6 %collective-permute-start.3 = (f32[1,128,256]{2,1,0:T(8,128)S(1)}, f32[1,128,256]{2,1,0:T(8,128)S(1)}, u32[]{:S(2)}, u32[]{:S(2)}) collective-permute-start(f32[1,128,256]{2,1,0:T(8,128)S(1)} %get-tuple-element.329), channel_id=1, source_target_pairs={{0,2},{2,4},{4,6},{6,8},{8,10},{10,12},{12,14},{14,16},{16,18},{18... | collective-permute-start | bytes 393224 | tf_op jit(solution)/shard_map/ppermute | solution.py:49
  2.2 9.0 %collective-permute-start.4 = (f32[1,128,256]{2,1,0:T(8,128)S(1)}, f32[1,128,256]{2,1,0:T(8,128)S(1)}, u32[]{:S(2)}, u32[]{:S(2)}) collective-permute-start(f32[1,128,256]{2,1,0:T(8,128)S(1)} %get-tuple-element.330), channel_id=1, source_target_pairs={{2,0},{4,2},{6,4},{8,6},{10,8},{12,10},{14,12},{16,14},{18,16},{20... | collective-permute-start | bytes 393224 | tf_op jit(solution)/shard_map/ppermute | solution.py:50
  7.3 3.6 %collective-permute-start.2 = (s32[1,256]{1,0:T(1,128)S(1)}, s32[1,256]{1,0:T(1,128)S(1)}, u32[]{:S(2)}, u32[]{:S(2)}) collective-permute-start(s32[1,256]{1,0:T(1,128)S(1)} %slice_bitcast_fusion.4), channel_id=1, source_target_pairs={{0,1},{1,0},{2,3},{3,2},{4,5},{5,4},{6,7},{7,6},{8,9},{9,8},{10,11... | collective-permute-start | bytes 3080 | tf_op jit(solution)/shard_map/ppermute | solution.py:57
  10.8 1.0 copy-start.1
  12.9 3.7 %collective-permute-start.5 = (f32[2,1,256]{2,1,0:T(1,128)S(1)}, f32[2,1,256]{2,1,0:T(1,128)S(1)}, u32[]{:S(2)}, u32[]{:S(2)}) collective-permute-start(f32[2,1,256]{2,1,0:T(1,128)S(1)} %get-tuple-element.313), channel_id=1, source_target_pairs={{0,1},{1,0},{2,3},{3,2},{4,5},{5,4},{6,7},{7,6},{8,9},{9,8},{10,11... | collective-permute-start | bytes 6152 | tf_op jit(solution)/shard_map/ppermute | solution.py:49
  14.9 3.6 %collective-permute-start.6 = (f32[2,1,256]{2,1,0:T(1,128)S(1)}, f32[2,1,256]{2,1,0:T(1,128)S(1)}, u32[]{:S(2)}, u32[]{:S(2)}) collective-permute-start(f32[2,1,256]{2,1,0:T(1,128)S(1)} %get-tuple-element.314), channel_id=1, source_target_pairs={{1,0},{0,1},{3,2},{2,3},{5,4},{4,5},{7,6},{6,7},{9,8},{8,9},{11,10... | collective-permute-start | bytes 6152 | tf_op jit(solution)/shard_map/ppermute | solution.py:50
  18.6 7.2 %collective-permute-start.7 = (f32[1,128,256]{2,1,0:T(8,128)S(1)}, f32[1,128,256]{2,1,0:T(8,128)S(1)}, u32[]{:S(2)}, u32[]{:S(2)}) collective-permute-start(f32[1,128,256]{2,1,0:T(8,128)S(1)} %get-tuple-element.311), channel_id=1, source_target_pairs={{0,2},{2,4},{4,6},{6,8},{8,10},{10,12},{12,14},{14,16},{16,18},{18... | collective-permute-start | bytes 393224 | tf_op jit(solution)/shard_map/ppermute | solution.py:57
  25.9 2.6 %collective-permute-start.8 = (f32[1,128,256]{2,1,0:T(8,128)S(1)}, f32[1,128,256]{2,1,0:T(8,128)S(1)}, u32[]{:S(2)}, u32[]{:S(2)}) collective-permute-start(f32[1,128,256]{2,1,0:T(8,128)S(1)} %get-tuple-element.310), channel_id=1, source_target_pairs={{0,30},{2,0},{4,2},{6,4},{8,6},{10,8},{12,10},{14,12},{16,14},{18,... | collective-permute-start | bytes 393224 | tf_op jit(solution)/shard_map/ppermute | solution.py:57
  28.5 3.7 %collective-permute-start.10 = (f32[2,1,256]{2,1,0:T(1,128)S(1)}, f32[2,1,256]{2,1,0:T(1,128)S(1)}, u32[]{:S(2)}, u32[]{:S(2)}) collective-permute-start(f32[2,1,256]{2,1,0:T(1,128)S(1)} %get-tuple-element.308), channel_id=1, source_target_pairs={{1,0},{0,1},{3,2},{2,3},{5,4},{4,5},{7,6},{6,7},{9,8},{8,9},{11,10... | collective-permute-start | bytes 6152 | tf_op jit(solution)/shard_map/ppermute | solution.py:50
  28.7 3.6 %collective-permute-start.9 = (f32[2,1,256]{2,1,0:T(1,128)S(1)}, f32[2,1,256]{2,1,0:T(1,128)S(1)}, u32[]{:S(2)}, u32[]{:S(2)}) collective-permute-start(f32[2,1,256]{2,1,0:T(1,128)S(1)} %get-tuple-element.307), channel_id=1, source_target_pairs={{0,1},{1,0},{2,3},{3,2},{4,5},{5,4},{6,7},{7,6},{8,9},{9,8},{10,11... | collective-permute-start | bytes 6152 | tf_op jit(solution)/shard_map/ppermute | solution.py:49
  33.1 1.0 copy-start.4
  35.3 14.7 %all-to-all-start = ((f32[2,128,256]{2,0,1:T(2,128)}), f32[2,128,256]{2,0,1:T(2,128)S(1)}, u32[]{:S(2)}, u32[]{:S(2)}) async-start(f32[2,128,256]{2,0,1:T(2,128)} %copy.87), calls=%async_computation | async-start | bytes 524288 | tf_op jit(solution)/shard_map/all_to_all | solution.py:150
  51.6 13.5 %all-to-all-start.1 = ((f32[32,8,256]{2,1,0:T(8,128)}), f32[32,8,256]{2,1,0:T(8,128)S(1)}, u32[]{:S(2)}, u32[]{:S(2)}) async-start(f32[32,8,256]{2,1,0:T(8,128)} %copy.90), calls=%async_computation.1 | async-start | bytes 524288 | tf_op jit(solution)/shard_map/all_to_all | solution.py:151
  65.3 3.8 %collective-permute-start = (f32[2,2,4,256]{3,2,1,0:T(4,128)S(1)}, f32[2,2,4,256]{3,2,1,0:T(4,128)S(1)}, u32[]{:S(2)}, u32[]{:S(2)}) collective-permute-start(f32[2,2,4,256]{3,2,1,0:T(4,128)S(1)} %get-tuple-element.420), channel_id=1, source_target_pairs={{1,0},{0,1},{3,2},{2,3},{5,4},{4,5},{7,6},{6,7},{9,8},{8,9},{11,10... | collective-permute-start | bytes 49160 | tf_op jit(solution)/shard_map/while/body/eval_jaxpr/ppermute | solution.py:50
  67.0 3.7 %collective-permute-start.1 = (f32[2,2,4,256]{3,2,1,0:T(4,128)S(1)}, f32[2,2,4,256]{3,2,1,0:T(4,128)S(1)}, u32[]{:S(2)}, u32[]{:S(2)}) collective-permute-start(f32[2,2,4,256]{3,2,1,0:T(4,128)S(1)} %get-tuple-element.421), channel_id=1, source_target_pairs={{0,1},{1,0},{2,3},{3,2},{4,5},{5,4},{6,7},{7,6},{8,9},{9,8},{10,11... | collective-permute-start | bytes 49160 | tf_op jit(solution)/shard_map/while/body/eval_jaxpr/ppermute | solution.py:49
  73.0 3.8 %collective-permute-start = (f32[2,2,4,256]{3,2,1,0:T(4,128)S(1)}, f32[2,2,4,256]{3,2,1,0:T(4,128)S(1)}, u32[]{:S(2)}, u32[]{:S(2)}) collective-permute-start(f32[2,2,4,256]{3,2,1,0:T(4,128)S(1)} %get-tuple-element.420), channel_id=1, source_target_pairs={{1,0},{0,1},{3,2},{2,3},{5,4},{4,5},{7,6},{6,7},{9,8},{8,9},{11,10... | collective-permute-start | bytes 49160 | tf_op jit(solution)/shard_map/while/body/eval_jaxpr/ppermute | solution.py:50
  73.4 3.7 %collective-permute-start.1 = (f32[2,2,4,256]{3,2,1,0:T(4,128)S(1)}, f32[2,2,4,256]{3,2,1,0:T(4,128)S(1)}, u32[]{:S(2)}, u32[]{:S(2)}) collective-permute-start(f32[2,2,4,256]{3,2,1,0:T(4,128)S(1)} %get-tuple-element.421), channel_id=1, source_target_pairs={{0,1},{1,0},{2,3},{3,2},{4,5},{5,4},{6,7},{7,6},{8,9},{9,8},{10,11... | collective-permute-start | bytes 49160 | tf_op jit(solution)/shard_map/while/body/eval_jaxpr/ppermute | solution.py:49
  79.3 3.8 %collective-permute-start = (f32[2,2,4,256]{3,2,1,0:T(4,128)S(1)}, f32[2,2,4,256]{3,2,1,0:T(4,128)S(1)}, u32[]{:S(2)}, u32[]{:S(2)}) collective-permute-start(f32[2,2,4,256]{3,2,1,0:T(4,128)S(1)} %get-tuple-element.420), channel_id=1, source_target_pairs={{1,0},{0,1},{3,2},{2,3},{5,4},{4,5},{7,6},{6,7},{9,8},{8,9},{11,10... | collective-permute-start | bytes 49160 | tf_op jit(solution)/shard_map/while/body/eval_jaxpr/ppermute | solution.py:50
  81.1 3.7 %collective-permute-start.1 = (f32[2,2,4,256]{3,2,1,0:T(4,128)S(1)}, f32[2,2,4,256]{3,2,1,0:T(4,128)S(1)}, u32[]{:S(2)}, u32[]{:S(2)}) collective-permute-start(f32[2,2,4,256]{3,2,1,0:T(4,128)S(1)} %get-tuple-element.421), channel_id=1, source_target_pairs={{0,1},{1,0},{2,3},{3,2},{4,5},{5,4},{6,7},{7,6},{8,9},{9,8},{10,11... | collective-permute-start | bytes 49160 | tf_op jit(solution)/shard_map/while/body/eval_jaxpr/ppermute | solution.py:49
  87.0 3.8 %collective-permute-start = (f32[2,2,4,256]{3,2,1,0:T(4,128)S(1)}, f32[2,2,4,256]{3,2,1,0:T(4,128)S(1)}, u32[]{:S(2)}, u32[]{:S(2)}) collective-permute-start(f32[2,2,4,256]{3,2,1,0:T(4,128)S(1)} %get-tuple-element.420), channel_id=1, source_target_pairs={{1,0},{0,1},{3,2},{2,3},{5,4},{4,5},{7,6},{6,7},{9,8},{8,9},{11,10... | collective-permute-start | bytes 49160 | tf_op jit(solution)/shard_map/while/body/eval_jaxpr/ppermute | solution.py:50
  87.4 3.7 %collective-permute-start.1 = (f32[2,2,4,256]{3,2,1,0:T(4,128)S(1)}, f32[2,2,4,256]{3,2,1,0:T(4,128)S(1)}, u32[]{:S(2)}, u32[]{:S(2)}) collective-permute-start(f32[2,2,4,256]{3,2,1,0:T(4,128)S(1)} %get-tuple-element.421), channel_id=1, source_target_pairs={{0,1},{1,0},{2,3},{3,2},{4,5},{5,4},{6,7},{7,6},{8,9},{9,8},{10,11... | collective-permute-start | bytes 49160 | tf_op jit(solution)/shard_map/while/body/eval_jaxpr/ppermute | solution.py:49
  93.4 3.8 %collective-permute-start = (f32[2,2,4,256]{3,2,1,0:T(4,128)S(1)}, f32[2,2,4,256]{3,2,1,0:T(4,128)S(1)}, u32[]{:S(2)}, u32[]{:S(2)}) collective-permute-start(f32[2,2,4,256]{3,2,1,0:T(4,128)S(1)} %get-tuple-element.420), channel_id=1, source_target_pairs={{1,0},{0,1},{3,2},{2,3},{5,4},{4,5},{7,6},{6,7},{9,8},{8,9},{11,10... | collective-permute-start | bytes 49160 | tf_op jit(solution)/shard_map/while/body/eval_jaxpr/ppermute | solution.py:50
  95.1 3.7 %collective-permute-start.1 = (f32[2,2,4,256]{3,2,1,0:T(4,128)S(1)}, f32[2,2,4,256]{3,2,1,0:T(4,128)S(1)}, u32[]{:S(2)}, u32[]{:S(2)}) collective-permute-start(f32[2,2,4,256]{3,2,1,0:T(4,128)S(1)} %get-tuple-element.421), channel_id=1, source_target_pairs={{0,1},{1,0},{2,3},{3,2},{4,5},{5,4},{6,7},{7,6},{8,9},{9,8},{10,11... | collective-permute-start | bytes 49160 | tf_op jit(solution)/shard_map/while/body/eval_jaxpr/ppermute | solution.py:49
  101.1 3.8 %collective-permute-start = (f32[2,2,4,256]{3,2,1,0:T(4,128)S(1)}, f32[2,2,4,256]{3,2,1,0:T(4,128)S(1)}, u32[]{:S(2)}, u32[]{:S(2)}) collective-permute-start(f32[2,2,4,256]{3,2,1,0:T(4,128)S(1)} %get-tuple-element.420), channel_id=1, source_target_pairs={{1,0},{0,1},{3,2},{2,3},{5,4},{4,5},{7,6},{6,7},{9,8},{8,9},{11,10... | collective-permute-start | bytes 49160 | tf_op jit(solution)/shard_map/while/body/eval_jaxpr/ppermute | solution.py:50
  101.5 3.7 %collective-permute-start.1 = (f32[2,2,4,256]{3,2,1,0:T(4,128)S(1)}, f32[2,2,4,256]{3,2,1,0:T(4,128)S(1)}, u32[]{:S(2)}, u32[]{:S(2)}) collective-permute-start(f32[2,2,4,256]{3,2,1,0:T(4,128)S(1)} %get-tuple-element.421), channel_id=1, source_target_pairs={{0,1},{1,0},{2,3},{3,2},{4,5},{5,4},{6,7},{7,6},{8,9},{9,8},{10,11... | collective-permute-start | bytes 49160 | tf_op jit(solution)/shard_map/while/body/eval_jaxpr/ppermute | solution.py:49
  107.5 3.7 %collective-permute-start.11 = (f32[2,8,256]{2,1,0:T(8,128)S(1)}, f32[2,8,256]{2,1,0:T(8,128)S(1)}, u32[]{:S(2)}, u32[]{:S(2)}) collective-permute-start(f32[2,8,256]{2,1,0:T(8,128)S(1)} %get-tuple-element.291), channel_id=1, source_target_pairs={{0,2},{2,0},{4,6},{6,4},{8,10},{10,8},{12,14},{14,12},{16,18},{18,... | collective-permute-start | bytes 49160 | tf_op jit(solution)/shard_map/ppermute | solution.py:32
  107.6 4.2 %collective-permute-start.12 = (f32[2,8,256]{2,1,0:T(8,128)S(1)}, f32[2,8,256]{2,1,0:T(8,128)S(1)}, u32[]{:S(2)}, u32[]{:S(2)}) collective-permute-start(f32[2,8,256]{2,1,0:T(8,128)S(1)} %get-tuple-element.290), channel_id=1, source_target_pairs={{0,4},{2,6},{4,0},{6,2},{8,12},{10,14},{12,8},{14,10},{16,20},{18,... | collective-permute-start | bytes 49160 | tf_op jit(solution)/shard_map/ppermute | solution.py:32
  107.7 6.4 %collective-permute-start.13 = (f32[2,8,256]{2,1,0:T(8,128)S(1)}, f32[2,8,256]{2,1,0:T(8,128)S(1)}, u32[]{:S(2)}, u32[]{:S(2)}) collective-permute-start(f32[2,8,256]{2,1,0:T(8,128)S(1)} %get-tuple-element.289), channel_id=1, source_target_pairs={{0,6},{2,4},{4,2},{6,0},{8,14},{10,12},{12,10},{14,8},{16,22},{18,... | collective-permute-start | bytes 49160 | tf_op jit(solution)/shard_map/ppermute | solution.py:32
  109.5 5.7 %collective-permute-start.14 = (f32[2,8,256]{2,1,0:T(8,128)S(1)}, f32[2,8,256]{2,1,0:T(8,128)S(1)}, u32[]{:S(2)}, u32[]{:S(2)}) collective-permute-start(f32[2,8,256]{2,1,0:T(8,128)S(1)} %get-tuple-element.288), channel_id=1, source_target_pairs={{0,8},{2,10},{4,12},{6,14},{8,0},{10,2},{12,4},{14,6},{16,24},{18,... | collective-permute-start | bytes 49160 | tf_op jit(solution)/shard_map/ppermute | solution.py:32
  109.5 7.4 %collective-permute-start.15 = (f32[2,8,256]{2,1,0:T(8,128)S(1)}, f32[2,8,256]{2,1,0:T(8,128)S(1)}, u32[]{:S(2)}, u32[]{:S(2)}) collective-permute-start(f32[2,8,256]{2,1,0:T(8,128)S(1)} %get-tuple-element.287), channel_id=1, source_target_pairs={{0,10},{2,8},{4,14},{6,12},{8,2},{10,0},{12,6},{14,4},{16,26},{18,... | collective-permute-start | bytes 49160 | tf_op jit(solution)/shard_map/ppermute | solution.py:32
  111.2 6.3 %collective-permute-start.16 = (f32[2,8,256]{2,1,0:T(8,128)S(1)}, f32[2,8,256]{2,1,0:T(8,128)S(1)}, u32[]{:S(2)}, u32[]{:S(2)}) collective-permute-start(f32[2,8,256]{2,1,0:T(8,128)S(1)} %get-tuple-element.286), channel_id=1, source_target_pairs={{0,12},{2,14},{4,8},{6,10},{8,4},{10,6},{12,0},{14,2},{16,28},{18,... | collective-permute-start | bytes 49160 | tf_op jit(solution)/shard_map/ppermute | solution.py:32
  111.8 8.8 %collective-permute-start.17 = (f32[2,8,256]{2,1,0:T(8,128)S(1)}, f32[2,8,256]{2,1,0:T(8,128)S(1)}, u32[]{:S(2)}, u32[]{:S(2)}) collective-permute-start(f32[2,8,256]{2,1,0:T(8,128)S(1)} %get-tuple-element.285), channel_id=1, source_target_pairs={{0,14},{2,12},{4,10},{6,8},{8,6},{10,4},{12,2},{14,0},{16,30},{18,... | collective-permute-start | bytes 49160 | tf_op jit(solution)/shard_map/ppermute | solution.py:32
  114.1 7.6 %collective-permute-start.18 = (f32[2,8,256]{2,1,0:T(8,128)S(1)}, f32[2,8,256]{2,1,0:T(8,128)S(1)}, u32[]{:S(2)}, u32[]{:S(2)}) collective-permute-start(f32[2,8,256]{2,1,0:T(8,128)S(1)} %get-tuple-element.284), channel_id=1, source_target_pairs={{0,16},{2,18},{4,20},{6,22},{8,24},{10,26},{12,28},{14,30},{16,0},... | collective-permute-start | bytes 49160 | tf_op jit(solution)/shard_map/ppermute | solution.py:32
  115.2 9.2 %collective-permute-start.19 = (f32[2,8,256]{2,1,0:T(8,128)S(1)}, f32[2,8,256]{2,1,0:T(8,128)S(1)}, u32[]{:S(2)}, u32[]{:S(2)}) collective-permute-start(f32[2,8,256]{2,1,0:T(8,128)S(1)} %get-tuple-element.283), channel_id=1, source_target_pairs={{0,18},{2,16},{4,22},{6,20},{8,26},{10,24},{12,30},{14,28},{16,2},... | collective-permute-start | bytes 49160 | tf_op jit(solution)/shard_map/ppermute | solution.py:32
  116.9 9.1 %collective-permute-start.20 = (f32[2,8,256]{2,1,0:T(8,128)S(1)}, f32[2,8,256]{2,1,0:T(8,128)S(1)}, u32[]{:S(2)}, u32[]{:S(2)}) collective-permute-start(f32[2,8,256]{2,1,0:T(8,128)S(1)} %get-tuple-element.282), channel_id=1, source_target_pairs={{0,20},{2,22},{4,16},{6,18},{8,28},{10,30},{12,24},{14,26},{16,4},... | collective-permute-start | bytes 49160 | tf_op jit(solution)/shard_map/ppermute | solution.py:32
  117.5 11.5 %collective-permute-start.21 = (f32[2,8,256]{2,1,0:T(8,128)S(1)}, f32[2,8,256]{2,1,0:T(8,128)S(1)}, u32[]{:S(2)}, u32[]{:S(2)}) collective-permute-start(f32[2,8,256]{2,1,0:T(8,128)S(1)} %get-tuple-element.281), channel_id=1, source_target_pairs={{0,22},{2,20},{4,18},{6,16},{8,30},{10,28},{12,26},{14,24},{16,6},... | collective-permute-start | bytes 49160 | tf_op jit(solution)/shard_map/ppermute | solution.py:32
  120.7 8.4 %collective-permute-start.22 = (f32[2,8,256]{2,1,0:T(8,128)S(1)}, f32[2,8,256]{2,1,0:T(8,128)S(1)}, u32[]{:S(2)}, u32[]{:S(2)}) collective-permute-start(f32[2,8,256]{2,1,0:T(8,128)S(1)} %get-tuple-element.280), channel_id=1, source_target_pairs={{0,24},{2,26},{4,28},{6,30},{8,16},{10,18},{12,20},{14,22},{16,8},... | collective-permute-start | bytes 49160 | tf_op jit(solution)/shard_map/ppermute | solution.py:32
  121.7 7.4 %collective-permute-start.23 = (f32[2,8,256]{2,1,0:T(8,128)S(1)}, f32[2,8,256]{2,1,0:T(8,128)S(1)}, u32[]{:S(2)}, u32[]{:S(2)}) collective-permute-start(f32[2,8,256]{2,1,0:T(8,128)S(1)} %get-tuple-element.294), channel_id=1, source_target_pairs={{0,26},{2,24},{4,30},{6,28},{8,18},{10,16},{12,22},{14,20},{16,10}... | collective-permute-start | bytes 49160 | tf_op jit(solution)/shard_map/ppermute | solution.py:32
  124.4 6.5 %collective-permute-start.24 = (f32[2,8,256]{2,1,0:T(8,128)S(1)}, f32[2,8,256]{2,1,0:T(8,128)S(1)}, u32[]{:S(2)}, u32[]{:S(2)}) collective-permute-start(f32[2,8,256]{2,1,0:T(8,128)S(1)} %get-tuple-element.293), channel_id=1, source_target_pairs={{0,28},{2,30},{4,24},{6,26},{8,20},{10,22},{12,16},{14,18},{16,12}... | collective-permute-start | bytes 49160 | tf_op jit(solution)/shard_map/ppermute | solution.py:32
  126.0 5.9 %collective-permute-start.25 = (f32[2,8,256]{2,1,0:T(8,128)S(1)}, f32[2,8,256]{2,1,0:T(8,128)S(1)}, u32[]{:S(2)}, u32[]{:S(2)}) collective-permute-start(f32[2,8,256]{2,1,0:T(8,128)S(1)} %get-tuple-element.279), channel_id=1, source_target_pairs={{0,30},{2,28},{4,26},{6,24},{8,22},{10,20},{12,18},{14,16},{16,14}... | collective-permute-start | bytes 49160 | tf_op jit(solution)/shard_map/ppermute | solution.py:32
  147.1 21.3 %copy-start.2 = (f32[2,128,256]{2,1,0:T(8,128)}, f32[2,128,256]{2,1,0:T(8,128)S(1)}, u32[]{:S(2)}) copy-start(f32[2,128,256]{2,1,0:T(8,128)S(1)} %get-tuple-element.207) | copy-start | bytes 786436
  148.1 3.7 %collective-permute-start.26 = (f32[2,1,256]{2,1,0:T(1,128)S(1)}, f32[2,1,256]{2,1,0:T(1,128)S(1)}, u32[]{:S(2)}, u32[]{:S(2)}) collective-permute-start(f32[2,1,256]{2,1,0:T(1,128)S(1)} %get-tuple-element.265), channel_id=1, source_target_pairs={{0,1},{1,0},{2,3},{3,2},{4,5},{5,4},{6,7},{7,6},{8,9},{9,8},{10,11... | collective-permute-start | bytes 6152 | tf_op jit(solution)/shard_map/ppermute | solution.py:49
  149.8 3.6 %collective-permute-start.27 = (f32[2,1,256]{2,1,0:T(1,128)S(1)}, f32[2,1,256]{2,1,0:T(1,128)S(1)}, u32[]{:S(2)}, u32[]{:S(2)}) collective-permute-start(f32[2,1,256]{2,1,0:T(1,128)S(1)} %get-tuple-element.266), channel_id=1, source_target_pairs={{1,0},{0,1},{3,2},{2,3},{5,4},{4,5},{7,6},{6,7},{9,8},{8,9},{11,10... | collective-permute-start | bytes 6152 | tf_op jit(solution)/shard_map/ppermute | solution.py:50
  153.5 7.2 %collective-permute-start.28 = (f32[1,128,256]{2,1,0:T(8,128)S(1)}, f32[1,128,256]{2,1,0:T(8,128)S(1)}, u32[]{:S(2)}, u32[]{:S(2)}) collective-permute-start(f32[1,128,256]{2,1,0:T(8,128)S(1)} %get-tuple-element.263), channel_id=1, source_target_pairs={{0,2},{2,4},{4,6},{6,8},{8,10},{10,12},{12,14},{14,16},{16,18},{18... | collective-permute-start | bytes 393224 | tf_op jit(solution)/shard_map/ppermute | solution.py:57
  160.8 2.6 %collective-permute-start.29 = (f32[1,128,256]{2,1,0:T(8,128)S(1)}, f32[1,128,256]{2,1,0:T(8,128)S(1)}, u32[]{:S(2)}, u32[]{:S(2)}) collective-permute-start(f32[1,128,256]{2,1,0:T(8,128)S(1)} %get-tuple-element.262), channel_id=1, source_target_pairs={{0,30},{2,0},{4,2},{6,4},{8,6},{10,8},{12,10},{14,12},{16,14},{18,... | collective-permute-start | bytes 393224 | tf_op jit(solution)/shard_map/ppermute | solution.py:57
  163.4 3.7 %collective-permute-start.30 = (f32[2,1,256]{2,1,0:T(1,128)S(1)}, f32[2,1,256]{2,1,0:T(1,128)S(1)}, u32[]{:S(2)}, u32[]{:S(2)}) collective-permute-start(f32[2,1,256]{2,1,0:T(1,128)S(1)} %get-tuple-element.259), channel_id=1, source_target_pairs={{0,1},{1,0},{2,3},{3,2},{4,5},{5,4},{6,7},{7,6},{8,9},{9,8},{10,11... | collective-permute-start | bytes 6152 | tf_op jit(solution)/shard_map/ppermute | solution.py:49
  163.9 3.6 %collective-permute-start.31 = (f32[2,1,256]{2,1,0:T(1,128)S(1)}, f32[2,1,256]{2,1,0:T(1,128)S(1)}, u32[]{:S(2)}, u32[]{:S(2)}) collective-permute-start(f32[2,1,256]{2,1,0:T(1,128)S(1)} %get-tuple-element.260), channel_id=1, source_target_pairs={{1,0},{0,1},{3,2},{2,3},{5,4},{4,5},{7,6},{6,7},{9,8},{8,9},{11,10... | collective-permute-start | bytes 6152 | tf_op jit(solution)/shard_map/ppermute | solution.py:50
  (2 other events, 1.9 us)
